TPU v7x, 256 devices: a whole 4x4x8 slice. The times are simulated.
256 devices in a mesh: wide: 32 (over z, x_lo, core), req: 8 (over y, x_hi).
Axes of the slice: x: 4 (x_hi: 2, x_lo: 2; x = x_hi * 2 + x_lo), y: 4, z: 8, core: 2. Of those that a mesh axis runs over, the one named last changes fastest.
Arguments:
- x_in: bfloat16 [2048, 8192], P('req', 'wide'), may hold values from -6 to 6
- w_xz: bfloat16 [8192, 2, 16384], P('req', None, 'wide'), may hold values from -0.0625 to 0.0625
- w_dt: bfloat16 [8192, 256], P('req', 'wide'), may hold values from -0.0625 to 0.0625
- w_bc: bfloat16 [8192, 4096], P('req', 'wide'), may hold values from -0.0625 to 0.0625
- dt_bias: float32 [256], P('wide'), may hold values from -7 to -3
- a_log: float32 [256], P('wide'), may hold values from 0 to 2.77
- d_skip: float32 [256], P('wide'), may hold values from 0.5 to 1.5
- conv_x_w: float32 [4, 16384], P(None, 'wide'), may hold values from -3 to 3
- conv_x_b: float32 [16384], P('wide'), may hold values from -3 to 3
- conv_bc_w: float32 [4, 4096], P(None, 'wide'), may hold values from -3 to 3
- conv_bc_b: float32 [4096], P('wide'), may hold values from -3 to 3
- norm_gain: float32 [16384], P('wide'), may hold values from 0.5 to 1.5
- stretch_start: int32 [8, 2], P('req'), may hold values from 0 to 255, as said below
- prefix_len: int32 [16], P('req'), may hold values from 0 to 32768, as said below
- state_slot: int32 [16], replicated, may hold values from 0 to 63, as said below
- ssm_pool: float32 [64, 256, 64, 256], P('req', 'wide'), may hold values from -6 to 6
- conv_x_pool: bfloat16 [64, 3, 16384], P('req', None, 'wide'), may hold values from -6 to 6
- conv_bc_pool: bfloat16 [64, 3, 4096], P('req', None, 'wide'), may hold values from -6 to 6
Outputs:
- y_out: bfloat16 [2048, 16384], P('req', 'wide')
- new_state: float32 [16, 256, 64, 256], P('req', 'wide')
Inputs may be any that keep to these rules, and one draw needn't show every extreme that they name: `stretch_start`: each row is 0 first and rises strictly; the 2 requests of an index of req cover its 256 tokens in order. `prefix_len`: zero means no cached state; in every draw some request has zero and one has 32768. `state_slot`: distinct slots; slot s is owned by index s // 8 of req; owners hold very uneven numbers of the requested slots.
All inputs are finite; a program needn't handle non-finite values.
Results may differ from a plain program's by a relative error of at most 0.014.
Values may be sent and summed in bfloat16 or wider, within the bound.
A program may use at most 128 MiB of HBM per device.

v0:
```python
import jax
import jax.numpy as jnp
from jax import lax
from jax.sharding import PartitionSpec as P

HEADS = 256
HEAD_DIM = 64
GROUPS = 8
NORM_EPS = 1e-05


def partner_2(block, axis, bit):
    count = lax.axis_size(axis)
    route = []
    for low in range(count):
        high = low | 1 << bit
        if high != low and high < count:
            route += [(low, high), (high, low)]
    return lax.ppermute(block, axis, route)


def segments(starts, count_tok):
    position = jnp.arange(count_tok, dtype=jnp.int32)
    seg_ids = jnp.sum((position[:, None] >= starts[None, :]).astype(jnp.int32), 1) - 1
    member = seg_ids[:, None] == jnp.arange(starts.shape[0], dtype=jnp.int32)[None, :]
    offset = position - jnp.sum(jnp.where(member, starts[None, :], 0), 1)
    same_req = seg_ids[:, None] == seg_ids[None, :]
    causal = position[:, None] >= position[None, :]
    return (member.astype(jnp.float32), offset, (same_req & causal).astype(jnp.float32))


def causal_conv(inputs, cache, kernel, bias, member, offset):
    kernel_len = kernel.shape[0]
    count_tok, channels = inputs.shape
    count_req = cache.shape[0]
    history = jnp.dot(
        member,
        cache.reshape(count_req, (kernel_len - 1) * channels),
        precision=lax.Precision.HIGHEST,
    )
    history = history.reshape(count_tok, kernel_len - 1, channels)
    values = inputs.astype(jnp.float32)
    total = bias[None, :] + kernel[kernel_len - 1][None, :] * values
    for lag_step in range(1, kernel_len):
        shifted = jnp.concatenate(
            [jnp.zeros((lag_step, channels), jnp.float32), values[: count_tok - lag_step]], 0
        )
        earlier = jnp.zeros((count_tok, channels), jnp.float32)
        for slot_place in range(kernel_len - 1):
            hit_place = offset - lag_step + kernel_len - 1 == slot_place
            earlier = earlier + jnp.where(hit_place[:, None], history[:, slot_place], 0.0)
        chosen = jnp.where((offset >= lag_step)[:, None], shifted, earlier)
        total = total + kernel[kernel_len - 1 - lag_step][None, :] * chosen
    return jax.nn.silu(total).astype(jnp.bfloat16)


def mixer(inputs, dt_raw, b_maps, c_maps, start_state, member, mask, dt_bias, a_log, d_skip):
    high = lax.Precision.HIGHEST
    step_size = jax.nn.softplus(dt_raw.astype(jnp.float32) + dt_bias[None, :])
    decay_rate = step_size * (-jnp.exp(a_log))[None, :]
    cumulative = jnp.dot(mask, decay_rate, precision=high)
    scores = jnp.dot(c_maps, b_maps.T, preferred_element_type=jnp.float32)
    spread_gap = jnp.minimum(cumulative.T[:, :, None] - cumulative.T[:, None, :], 0.0)
    decay = jnp.exp(spread_gap) * mask[None] * step_size.T[:, None, :]
    weights = (decay * scores[None]).astype(jnp.bfloat16)
    intra = jnp.einsum("hts,shp->thp", weights, inputs, preferred_element_type=jnp.float32)
    values = inputs.astype(jnp.float32)
    from_state = jnp.einsum(
        "tn,jhpn->jthp", c_maps.astype(jnp.float32), start_state, precision=high
    )
    from_state = jnp.einsum("tj,jthp->thp", member, from_state, precision=high)
    from_state = from_state * jnp.exp(cumulative)[:, :, None]
    result = intra + from_state + d_skip[None, :, None] * values
    ends = jnp.dot(member.T, decay_rate, precision=high)
    to_end = jnp.exp(jnp.dot(member, ends, precision=high) - cumulative)
    carried = (to_end * step_size)[:, :, None] * values
    split_req = (member.T[:, :, None, None] * carried[None]).astype(jnp.bfloat16)
    fresh = jnp.einsum("jthp,tn->jhpn", split_req, b_maps, preferred_element_type=jnp.float32)
    final_state = jnp.exp(ends)[:, :, None, None] * start_state + fresh
    return (result, final_state)


def on_device(
    x_in,
    w_xz,
    w_dt,
    w_bc,
    dt_bias,
    a_log,
    d_skip,
    conv_x_w,
    conv_x_b,
    conv_bc_w,
    conv_bc_b,
    norm_gain,
    stretch_start,
    prefix_len,
    state_slot,
    ssm_pool,
    conv_x_pool,
    conv_bc_pool,
):
    features = lax.all_gather(x_in, "wide", axis=1, tiled=True)
    count_tok = features.shape[0]
    local_width = w_xz.shape[2]
    local_heads = w_dt.shape[1]
    acc_xz = jnp.einsum(
        "td,dkc->tkc",
        features,
        lax.all_gather(w_xz, "req", axis=0, tiled=True),
        preferred_element_type=jnp.float32,
    )
    acc_dt = jnp.dot(
        features,
        lax.all_gather(w_dt, "req", axis=0, tiled=True),
        preferred_element_type=jnp.float32,
    )
    acc_bc = jnp.dot(
        features,
        lax.all_gather(w_bc, "req", axis=0, tiled=True),
        preferred_element_type=jnp.float32,
    )
    proj_xz = acc_xz.astype(jnp.bfloat16)
    dt_raw = acc_dt.astype(jnp.bfloat16)
    bc_raw = acc_bc.astype(jnp.bfloat16)
    owner = lax.axis_index("req")
    req_count = lax.axis_size("req")
    slot_count = conv_x_pool.shape[0]
    local_slot = jnp.clip(state_slot - owner * slot_count, 0, slot_count - 1)
    is_owner = state_slot // slot_count == owner
    send_ssm = jnp.where(is_owner[:, None, None, None], ssm_pool[local_slot], 0.0)
    send_cx = jnp.where(is_owner[:, None, None], conv_x_pool[local_slot].astype(jnp.float32), 0.0)
    send_cbc = jnp.where(is_owner[:, None, None], conv_bc_pool[local_slot].astype(jnp.float32), 0.0)
    got_ssm, got_cx, got_cbc = (
        lax.all_to_all(send_ssm, "req", split_axis=0, concat_axis=0, tiled=True),
        lax.all_to_all(send_cx, "req", split_axis=0, concat_axis=0, tiled=True),
        lax.all_to_all(send_cbc, "req", split_axis=0, concat_axis=0, tiled=True),
    )
    group_reqs = prefix_len.shape[0]
    has_cache = (prefix_len > 0).astype(jnp.float32)
    start_state = (
        jnp.sum(got_ssm.reshape((req_count, group_reqs) + got_ssm.shape[1:]), 0)
        * has_cache[:, None, None, None]
    )
    cache_x = (
        jnp.sum(got_cx.reshape((req_count, group_reqs) + got_cx.shape[1:]), 0)
        * has_cache[:, None, None]
    )
    cache_bc = (
        jnp.sum(got_cbc.reshape((req_count, group_reqs) + got_cbc.shape[1:]), 0)
        * has_cache[:, None, None]
    )
    member, offset, mask = segments(stretch_start[0], count_tok)
    x_conv = causal_conv(proj_xz[:, 1], cache_x, conv_x_w, conv_x_b, member, offset)
    bc_conv = causal_conv(bc_raw, cache_bc, conv_bc_w, conv_bc_b, member, offset)
    wide_index = lax.axis_index("wide")
    group_span = lax.axis_size("wide") // GROUPS
    bit_total = group_span.bit_length() - 1
    joined = bc_conv
    for bit_index in range(bit_total):
        partner = partner_2(joined, "wide", bit_index)
        upper_half = wide_index // (1 << bit_index) % 2 == 1
        joined = jnp.where(
            upper_half, jnp.concatenate([partner, joined], 1), jnp.concatenate([joined, partner], 1)
        )
    state_width = joined.shape[1] // 2
    b_maps = joined[:, :state_width]
    c_maps = joined[:, state_width:]
    head_width = local_width // local_heads
    result, final_state = mixer(
        x_conv.reshape(count_tok, local_heads, head_width),
        dt_raw,
        b_maps,
        c_maps,
        start_state,
        member,
        mask,
        dt_bias,
        a_log,
        d_skip,
    )
    gated = result.reshape(count_tok, local_width) * jax.nn.silu(proj_xz[:, 0].astype(jnp.float32))
    square_sum = jnp.sum(gated * gated, 1)
    for bit_index in range(bit_total):
        square_sum = square_sum + partner_2(square_sum, "wide", bit_index)
    mean_sq = square_sum / (HEADS * HEAD_DIM // GROUPS)
    normed = gated * lax.rsqrt(mean_sq + NORM_EPS)[:, None] * norm_gain[None, :]
    return (normed.astype(jnp.bfloat16), final_state)


def solution(mesh):
    in_specs = (
        P("req", "wide"),
        P("req", None, "wide"),
        P("req", "wide"),
        P("req", "wide"),
        P("wide"),
        P("wide"),
        P("wide"),
        P(None, "wide"),
        P("wide"),
        P(None, "wide"),
        P("wide"),
        P("wide"),
        P("req", None),
        P("req"),
        P(),
        P("req", "wide", None, None),
        P("req", None, "wide"),
        P("req", None, "wide"),
    )
    out_specs = (P("req", "wide"), P("req", "wide", None, None))
    return jax.shard_map(
        on_device, mesh=mesh, in_specs=in_specs, out_specs=out_specs, check_vma=False
    )
```

profile of v0, /device:TPU:1, one launch (start us, length us, event | category | flops | bytes accessed | tf_op | source)
XLA Modules:
  0.0 421.8 jit_solution(5018810072848733110)
XLA Ops:
  7.2 0.0 copy-start
  7.2 0.0 all-gather.8.cloned.1.call-start
  7.2 0.7 all-gather.8.cloned.1.call-update
  7.9 0.0 all-gather.4.cloned.1.call-start
  8.0 0.7 all-gather.4.cloned.1.call-update
  8.7 0.0 all-gather.6.cloned.1.call-start
  8.7 3.2 copy.42
  12.0 0.0 all-gather.6.cloned.1.call-update
  12.0 0.6 gather_fusion.1
  12.7 0.1 convert_select_fusion.1
  12.7 0.6 copy.47
  13.4 7.5 %all-to-all-start.1 = ((f32[16,3,128]{2,1,0:T(4,128)}), f32[16,3,128]{2,1,0:T(4,128)S(1)}, u32[]{:S(2)}, u32[]{:S(2)}) async-start(f32[16,3,128]{2,1,0:T(4,128)} %copy.47), calls=%async_computation.1 | async-start | bytes 65536 | tf_op jit(solution)/shard_map/all_to_all | solution.py:137
  20.9 0.7 gather_fusion
  21.6 0.1 convert_select_fusion
  21.6 0.7 copy.43
  22.4 6.5 %gather_fusion.2 = f32[16,8,64,256]{3,2,1,0:T(8,128)} fusion(f32[8,8,64,256]{3,2,1,0:T(8,128)} %param.33, s32[1024]{0:T(1024)S(1)} %pad_clamp_fusion), kind=kCustom, calls=%fused_computation.2 | custom fusion | bytes 16777280 | tf_op jit(solution)/shard_map/gather | solution.py:131
  28.9 6.6 %all-to-all-start = ((f32[16,3,512]{2,1,0:T(4,128)}), f32[16,3,512]{2,1,0:T(4,128)S(1)}, u32[]{:S(2)}, u32[]{:S(2)}) async-start(f32[16,3,512]{2,1,0:T(4,128)} %copy.43), calls=%async_computation | async-start | bytes 262144 | tf_op jit(solution)/shard_map/all_to_all | solution.py:136
  35.5 8.4 %broadcast_select_fusion = f32[16,8,64,256]{3,2,1,0:T(8,128)} fusion(f32[16,8,64,256]{3,2,1,0:T(8,128)} %gather_fusion.2, pred[16]{0:T(512)(128)(4,1)S(1)} %fusion.71), kind=kLoop, calls=%fused_computation.5 | loop fusion | flops 2097152 | bytes 16777232 | tf_op jit(solution)/shard_map/jit(_where)/select_n | solution.py:131
  44.0 0.0 copy-start.9
  44.0 6.8 %all-to-all-start.2 = ((f32[16,8,64,256]{3,2,1,0:T(8,128)}), f32[16,8,64,256]{3,2,1,0:T(8,128)}, u32[]{:S(2)}, u32[]{:S(2)}) async-start(f32[16,8,64,256]{3,2,1,0:T(8,128)} %broadcast_select_fusion), calls=%async_computation.2 | async-start | bytes 16777216 | tf_op jit(solution)/shard_map/all_to_all | solution.py:135
  50.8 137.9 %all_gather.14 = bf16[8192,8]{0,1:T(8,128)(2,1)S(1)} all-gather(bf16[1024,8]{0,1:T(8,128)(2,1)S(1)} %copy-done.4), channel_id=1, replica_groups=mesh['wide'=32,'req'=8] {'req'}, dimensions={0}, use_global_device_ids=true | all-gather | bytes 147456 | tf_op jit(solution)/shard_map/all_gather | solution.py:115
  188.7 0.1 fusion.64
  188.8 0.1 select_reduce_fusion
  189.0 0.8 fusion.36
  189.8 0.4 fusion.57
  190.3 0.1 broadcast_multiply_fusion
  190.4 0.8 fusion.59
  191.2 4.3 %reduce_sum.64 = f32[2,8,64,256]{3,2,1,0:T(8,128)S(1)} reduce(f32[8,2,8,64,256]{4,3,2,1,0:T(8,128)} %bitcast.33, f32[]{:T(128)} %constant.94.clone.1), dimensions={0}, to_apply=%region_4.5 | reduce | flops 1835008 | bytes 9437188 | tf_op jit(solution)/shard_map/reduce_sum | solution.py:142
  195.5 0.0 copy-start.10
  195.5 0.0 all-gather.8.cloned.1.call-done
  195.5 2.7 all-gather.4.cloned.1.call-done
  198.2 4.5 %fusion.7 = f32[256,128]{0,1:T(8,128)S(1)} fusion(bf16[256,8192]{1,0:T(8,128)(2,1)} %all-gather.4.cloned.1.call-done, bf16[8192,128]{1,0:T(8,128)(2,1)} %all-gather.8.cloned.1.call-done), kind=kOutput, calls=%fused_computation.13 | convolution fusion | flops 536936448 | bytes 6422528 | tf_op jit(solution)/shard_map/dot_general | solution.py:118
  202.8 0.3 multiply_convert_fusion.5
  203.1 5.2 %collective-permute-start = (bf16[256,128]{0,1:T(8,128)(2,1)S(1)}, bf16[256,128]{0,1:T(8,128)(2,1)S(1)}, u32[]{:S(2)}, u32[]{:S(2)}) collective-permute-start(bf16[256,128]{0,1:T(8,128)(2,1)S(1)} %multiply_convert_fusion.5), channel_id=1, source_target_pairs={{0,8},{8,0},{16,24},{24,16},{32,40},{40,32},{48,56},{56,48},{64,72... | collective-permute-start | bytes 196616 | tf_op jit(solution)/shard_map/ppermute | solution.py:19
  208.2 1.2 compare_select_fusion
  209.4 0.3 fusion.76
  209.7 0.3 fusion.77
  210.0 0.1 maximum_select_fusion.1
  210.0 0.3 collective-permute-start.1
  210.3 0.2 fusion.9
  210.5 4.8 %collective-permute-done.1 = bf16[256,256]{0,1:T(8,128)(2,1)S(1)} collective-permute-done((bf16[256,256]{0,1:T(8,128)(2,1)S(1)}, bf16[256,256]{0,1:T(8,128)(2,1)S(1)}, u32[]{:S(2)}, u32[]{:S(2)}) %collective-permute-start.1) | collective-permute-done | bytes 131104 | tf_op jit(solution)/shard_map/ppermute | solution.py:19
  215.3 0.1 maximum_select_fusion
  215.4 0.7 fusion.19
  216.1 0.9 fusion.12
  217.1 0.9 fusion.44
  218.0 168.4 %all-gather.6.cloned.1.call-done = bf16[8192,2,512]{2,0,1:T(8,128)(2,1)} async-done(((bf16[1024,2,512]{2,0,1:T(8,128)(2,1)}), bf16[8192,2,512]{2,0,1:T(8,128)(2,1)}) %all-gather.6.cloned.1.call-update) | async-done | bytes 16777232 | tf_op jit(solution)/shard_map/all_gather | solution.py:110
  386.4 11.5 %fusion.2 = bf16[256,2,512]{2,0,1:T(8,128)(2,1)S(1)} fusion(bf16[8192,2,512]{2,0,1:T(8,128)(2,1)} %all-gather.6.cloned.1.call-done, bf16[256,8192]{1,0:T(8,128)(2,1)} %all-gather.4.cloned.1.call-done), kind=kOutput, calls=%fused_computation.8 | convolution fusion | flops 4295229440 | bytes 21495808 | tf_op jit(solution)/shard_map/td,dkc->tkc/dot_general | solution.py:107
  397.9 0.0 copy-start.6
  397.9 0.9 slice_convert_fusion
  398.8 0.8 slice_bitcast_fusion
  399.6 0.8 slice_bitcast_fusion.1
  400.4 0.8 slice_bitcast_fusion.5
  401.3 2.0 copy.52
  403.3 3.0 multiply_convert_fusion.4
  406.3 1.1 copy.46
  407.4 0.0 copy-start.7
  407.4 2.2 multiply_reduce_fusion
  409.7 1.5 collective-permute-start.2
  411.2 0.8 collective-permute-done.2
  412.0 0.3 collective-permute-start.3
  412.3 1.3 convolution_add_fusion
  413.6 0.2 copy.51
  413.8 0.6 collective-permute-done.3
  414.4 0.9 fusion.34
  (48 shorter events, 0.3 us)
Async XLA Ops:
  7.2 13.7 %copy-start = (bf16[8,3,512]{2,0,1:T(8,128)(2,1)S(1)}, bf16[8,3,512]{2,0,1:T(8,128)(2,1)}, u32[]{:S(2)}) copy-start(bf16[8,3,512]{2,0,1:T(8,128)(2,1)} %param.34) | copy-start | bytes 73732
  7.2 4.8 %copy-start.12 = (s32[16]{0:T(128)S(1)}, s32[16]{0:T(128)}, u32[]{:S(2)}) copy-start(s32[16]{0:T(128)} %param.32) | copy-start | bytes 196
  7.2 4.8 %copy-start.3 = (bf16[8,3,128]{2,0,1:T(8,128)(2,1)S(1)}, bf16[8,3,128]{2,0,1:T(8,128)(2,1)}, u32[]{:S(2)}) copy-start(bf16[8,3,128]{2,0,1:T(8,128)(2,1)} %param.35) | copy-start | bytes 18436
  7.2 188.3 %all-gather.8.cloned.1.call-start = ((), (), s32[]{:S(2)}) async-start(), calls=%async_computation.5 | async-start | bytes 2359296 | tf_op jit(solution)/shard_map/all_gather | solution.py:120
  7.9 190.3 %all-gather.4.cloned.1.call-start = ((), (), s32[]{:S(2)}) async-start(), calls=%async_computation.3 | async-start | bytes 4325376 | tf_op jit(solution)/shard_map/all_gather | solution.py:103
  8.7 377.7 %all-gather.6.cloned.1.call-start = ((), (), s32[]{:S(2)}) async-start(), calls=%async_computation.4 | async-start | bytes 18874368 | tf_op jit(solution)/shard_map/all_gather | solution.py:110
  13.4 15.5 %all-to-all-start.1 = ((f32[16,3,128]{2,1,0:T(4,128)}), f32[16,3,128]{2,1,0:T(4,128)S(1)}, u32[]{:S(2)}, u32[]{:S(2)}) async-start(f32[16,3,128]{2,1,0:T(4,128)} %copy.47), calls=%async_computation.1 | async-start | bytes 65536 | tf_op jit(solution)/shard_map/all_to_all | solution.py:137
  28.9 15.1 %all-to-all-start = ((f32[16,3,512]{2,1,0:T(4,128)}), f32[16,3,512]{2,1,0:T(4,128)S(1)}, u32[]{:S(2)}, u32[]{:S(2)}) async-start(f32[16,3,512]{2,1,0:T(4,128)} %copy.43), calls=%async_computation | async-start | bytes 262144 | tf_op jit(solution)/shard_map/all_to_all | solution.py:136
  44.0 6.8 %copy-start.4 = (bf16[1024,8]{0,1:T(8,128)(2,1)S(1)}, bf16[1024,8]{0,1:T(8,128)(2,1)}, u32[]{:S(2)}) copy-start(bf16[1024,8]{0,1:T(8,128)(2,1)} %param.20) | copy-start | bytes 49156
  44.0 144.7 %copy-start.11 = (s32[1,2]{1,0:T(1,128)S(1)}, s32[1,2]{1,0:T(1,128)}, u32[]{:S(2)}) copy-start(s32[1,2]{1,0:T(1,128)} %param.30) | copy-start | bytes 28
  44.0 144.9 %copy-start.13 = (s32[2]{0:T(128)S(1)}, s32[2]{0:T(128)}, u32[]{:S(2)}) copy-start(s32[2]{0:T(128)} %param.31) | copy-start | bytes 28
  44.0 144.9 %copy-start.14 = (f32[8]{0:T(128)S(1)}, f32[8]{0:T(128)}, u32[]{:S(2)}) copy-start(f32[8]{0:T(128)} %param.23) | copy-start | bytes 100
  44.0 144.9 %copy-start.9 = (f32[4,128]{1,0:T(4,128)S(1)}, f32[4,128]{1,0:T(4,128)}, u32[]{:S(2)}) copy-start(f32[4,128]{1,0:T(4,128)} %param.27) | copy-start | bytes 6148
  44.0 144.9 %copy-start.5 = (f32[4,512]{1,0:T(4,128)S(1)}, f32[4,512]{1,0:T(4,128)}, u32[]{:S(2)}) copy-start(f32[4,512]{1,0:T(4,128)} %param.25) | copy-start | bytes 24580
  44.0 147.2 %all-to-all-start.2 = ((f32[16,8,64,256]{3,2,1,0:T(8,128)}), f32[16,8,64,256]{3,2,1,0:T(8,128)}, u32[]{:S(2)}, u32[]{:S(2)}) async-start(f32[16,8,64,256]{3,2,1,0:T(8,128)} %broadcast_select_fusion), calls=%async_computation.2 | async-start | bytes 16777216 | tf_op jit(solution)/shard_map/all_to_all | solution.py:135
  195.5 7.2 %copy-start.10 = (f32[128]{0:T(128)S(1)}, f32[128]{0:T(128)}, u32[]{:S(2)}) copy-start(f32[128]{0:T(128)} %param.28) | copy-start | bytes 1540
  195.5 12.7 %copy-start.8 = (f32[8]{0:T(128)S(1)}, f32[8]{0:T(128)}, u32[]{:S(2)}) copy-start(f32[8]{0:T(128)} %param.22) | copy-start | bytes 100
  198.2 10.0 %copy-start.2 = (bf16[256,8192]{1,0:T(8,128)(2,1)S(1)}, bf16[256,8192]{1,0:T(8,128)(2,1)}, u32[]{:S(2)}) copy-start(bf16[256,8192]{1,0:T(8,128)(2,1)} %all-gather.4.cloned.1.call-done) | copy-start | bytes 12582916
  203.1 6.9 %collective-permute-start = (bf16[256,128]{0,1:T(8,128)(2,1)S(1)}, bf16[256,128]{0,1:T(8,128)(2,1)S(1)}, u32[]{:S(2)}, u32[]{:S(2)}) collective-permute-start(bf16[256,128]{0,1:T(8,128)(2,1)S(1)} %multiply_convert_fusion.5), channel_id=1, source_target_pairs={{0,8},{8,0},{16,24},{24,16},{32,40},{40,32},{48,56},{56,48},{64,72... | collective-permute-start | bytes 196616 | tf_op jit(solution)/shard_map/ppermute | solution.py:19
  210.0 5.3 %collective-permute-start.1 = (bf16[256,256]{0,1:T(8,128)(2,1)S(1)}, bf16[256,256]{0,1:T(8,128)(2,1)S(1)}, u32[]{:S(2)}, u32[]{:S(2)}) collective-permute-start(bf16[256,256]{0,1:T(8,128)(2,1)S(1)} %maximum_select_fusion.1), channel_id=1, source_target_pairs={{0,16},{16,0},{8,24},{24,8},{32,48},{48,32},{40,56},{56,40},{64,80... | collective-permute-start | bytes 393224 | tf_op jit(solution)/shard_map/ppermute | solution.py:19
  397.9 5.4 %copy-start.6 = (f32[512]{0:T(512)S(1)}, f32[512]{0:T(512)}, u32[]{:S(2)}) copy-start(f32[512]{0:T(512)} %param.26) | copy-start | bytes 6148
  398.8 8.6 %copy-start.15 = (f32[8]{0:T(128)S(1)}, f32[8]{0:T(128)}, u32[]{:S(2)}) copy-start(f32[8]{0:T(128)} %param.24) | copy-start | bytes 100
  407.4 7.0 %copy-start.7 = (f32[512]{0:T(512)S(1)}, f32[512]{0:T(512)}, u32[]{:S(2)}) copy-start(f32[512]{0:T(512)} %param.29) | copy-start | bytes 6148
  407.4 7.9 %copy-start.1 = (bf16[8,3,512]{2,0,1:T(8,128)(2,1)S(1)}, bf16[8,3,512]{2,0,1:T(8,128)(2,1)}, u32[]{:S(2)}) copy-start(bf16[8,3,512]{2,0,1:T(8,128)(2,1)} %param.34) | copy-start | bytes 73732
  409.7 2.3 collective-permute-start.2
  412.0 2.4 collective-permute-start.3
Sparse Core Ops, SparseCore 0:
  10.7 75.4 all-gather.7
  87.9 110.2 all-gather.3
  200.8 185.4 all-gather.5
where the time goes:
time: 422 us
  waiting for transfers between devices  179 us (42%)
  blocking collectives  138 us (33%)
  starting transfers between devices  28.2 us (7%)
  matrix products  24.4 us (6%)
  other arithmetic  20.2 us (5%)
  local copies, waits for them, and re-layouts  18.4 us (4%)
  between operations  14.1 us (3%)
    all_gather x1, waiting for transfers between devices, on_device(): lax.all_gather(w_xz, 'req', axis=0, tiled=True)  168 us
    all_gather x1, blocking collectives, on_device(): lax.all_gather(w_dt, 'req', axis=0, tiled=True)  138 us
    dot_general x1, matrix products, on_device(): jnp.einsum('td,dkc->tkc', features, lax.all_gather(w_xz, 'req', axis=0, t...  11.5 us
    select_n x1, other arithmetic, on_device(): jnp.where(is_owner[:, None, None, None], ssm_pool[local_slot], 0.0)  8.44 us
  transfers between devices with their start and end apart: 10, of which 5 were waited for; matrix products, arithmetic and copies ran while one was open for 9% of the time, Pallas kernels for 0%

commit v1 on v0

--- a/solution.py
+++ b/solution.py
@@ -107,7 +107,9 @@
     acc_xz = jnp.einsum(
         "td,dkc->tkc",
         features,
-        lax.all_gather(w_xz, "req", axis=0, tiled=True),
+        jnp.concatenate(
+            lax.all_to_all(jnp.stack([w_xz] * lax.axis_size("req")), "req", 0, 0), axis=0
+        ),
         preferred_element_type=jnp.float32,
     )
     acc_dt = jnp.dot(

time: 422 us -> 483 us (1.14)
  blocking collectives: 138 us -> 217 us
  waiting for transfers between devices: 179 us -> 150 us
  local copies, waits for them, and re-layouts: 18.4 us -> 31.9 us
  matrix products: 24.4 us -> 17.4 us
    all_gather x1 -> x0, waiting for transfers between devices: 168 us -> none  [on_device(): lax.all_gather(w_xz, 'req', axis=0, tiled=True)]
    all_to_all x1, waiting for transfers between devices: 0.01 us -> 92 us  [on_device(): lax.all_to_all(send_ssm, 'req', split_axis=0, concat_axis=0, tiled=True)]
    all_gather x1, blocking collectives: 138 us -> 217 us  [on_device(): lax.all_gather(w_dt, 'req', axis=0, tiled=True)]
    all_gather x1, waiting for transfers between devices: 2.68 us -> 51.7 us  [on_device(): features = lax.all_gather(x_in, 'wide', axis=1, tiled=True)]
    all_to_all x0 -> x1, local copies, waits for them, and re-layouts: none -> 8.24 us  [on_device(): lax.all_to_all(jnp.stack([w_xz] * lax.axis_size('req')), 'req', 0, 0)]
    dot_general x1, matrix products: 11.5 us -> 4.52 us  [on_device(): jnp.einsum('td,dkc->tkc', features, jnp.concatenate(lax.all_to_all(jnp.st...]
    another operation x0 -> x1, local copies, waits for them, and re-layouts: none -> 5.89 us  [on_device(): jnp.stack([w_xz] * lax.axis_size('req'))]
    all_to_all x0 -> x1, starting transfers between devices: none -> 5.89 us  [on_device(): lax.all_to_all(jnp.stack([w_xz] * lax.axis_size('req')), 'req', 0, 0)]
  transfers between devices with their start and end apart: 10 -> 10, of which waited for: 5 -> 4; matrix products, arithmetic and copies ran while one was open for 9% -> 7% of each run, Pallas kernels for 0% -> 0%
where the time goes in v1:
time: 483 us; the launch traced here: 482 us
  blocking collectives  217 us (45%)
  waiting for transfers between devices  150 us (31%)
  local copies, waits for them, and re-layouts  31.9 us (7%)
  starting transfers between devices  30.4 us (6%)
  other arithmetic  21.5 us (4%)
  matrix products  17.4 us (4%)
  between operations  14.4 us (3%)
    all_gather x1, blocking collectives, on_device(): lax.all_gather(w_dt, 'req', axis=0, tiled=True)  217 us
    all_to_all x1, waiting for transfers between devices, on_device(): lax.all_to_all(send_ssm, 'req', split_axis=0, concat_axis=0, tiled=True)  92 us
    all_gather x1, waiting for transfers between devices, on_device(): features = lax.all_gather(x_in, 'wide', axis=1, tiled=True)  51.7 us
  transfers between devices with their start and end apart: 10, of which 4 were waited for; matrix products, arithmetic and copies ran while one was open for 7% of the time, Pallas kernels for 0%

profile of v1, /device:TPU:1, one launch (start us, length us, event | category | flops | bytes accessed | tf_op | source)
XLA Modules:
  0.0 482.3 jit_solution(16611814541089707031)
XLA Ops:
  7.2 0.0 copy-start
  7.2 0.7 fusion.71
  7.9 0.7 compare_select_fusion.2
  8.5 1.3 gather_fusion.1
  9.8 0.1 convert_select_fusion.1
  9.9 0.6 copy.48
  10.5 7.5 %all-to-all-start.2 = ((f32[16,3,128]{2,1,0:T(4,128)}), f32[16,3,128]{2,1,0:T(4,128)S(1)}, u32[]{:S(2)}, u32[]{:S(2)}) async-start(f32[16,3,128]{2,1,0:T(4,128)} %copy.48), calls=%async_computation.2 | async-start | bytes 65536 | tf_op jit(solution)/shard_map/all_to_all | solution.py:139
  18.0 0.7 gather_fusion
  18.7 0.1 convert_select_fusion
  18.8 0.7 copy.44
  19.5 6.5 %gather_fusion.2 = f32[16,8,64,256]{3,2,1,0:T(8,128)} fusion(f32[8,8,64,256]{3,2,1,0:T(8,128)} %param.33, s32[1024]{0:T(1024)S(1)} %pad_clamp_fusion), kind=kCustom, calls=%fused_computation.2 | custom fusion | bytes 16777280 | tf_op jit(solution)/shard_map/gather | solution.py:133
  26.0 6.6 %all-to-all-start.1 = ((f32[16,3,512]{2,1,0:T(4,128)}), f32[16,3,512]{2,1,0:T(4,128)S(1)}, u32[]{:S(2)}, u32[]{:S(2)}) async-start(f32[16,3,512]{2,1,0:T(4,128)} %copy.44), calls=%async_computation.1 | async-start | bytes 262144 | tf_op jit(solution)/shard_map/all_to_all | solution.py:138
  32.7 8.4 %broadcast_select_fusion = f32[16,8,64,256]{3,2,1,0:T(8,128)} fusion(f32[16,8,64,256]{3,2,1,0:T(8,128)} %gather_fusion.2, pred[16]{0:T(512)(128)(4,1)S(1)} %fusion.71), kind=kLoop, calls=%fused_computation.5 | loop fusion | flops 2097152 | bytes 16777232 | tf_op jit(solution)/shard_map/jit(_where)/select_n | solution.py:133
  41.1 6.6 %all-to-all-start.3 = ((f32[16,8,64,256]{3,2,1,0:T(8,128)}), f32[16,8,64,256]{3,2,1,0:T(8,128)}, u32[]{:S(2)}, u32[]{:S(2)}) async-start(f32[16,8,64,256]{3,2,1,0:T(8,128)} %broadcast_select_fusion), calls=%async_computation.3 | async-start | bytes 16777216 | tf_op jit(solution)/shard_map/all_to_all | solution.py:137
  47.7 1.9 copy.42
  49.7 92.0 %all-to-all-done.3 = f32[16,8,64,256]{3,2,1,0:T(8,128)} async-done(((f32[16,8,64,256]{3,2,1,0:T(8,128)}), f32[16,8,64,256]{3,2,1,0:T(8,128)}, u32[]{:S(2)}, u32[]{:S(2)}) %all-to-all-start.3) | async-done | bytes 8388640 | tf_op jit(solution)/shard_map/all_to_all | solution.py:137
  141.7 5.9 %stack.2 = bf16[8,1024,2,512]{3,1,2,0:T(8,128)(2,1)} broadcast(bf16[1024,2,512]{2,0,1:T(8,128)(2,1)S(1)} %copy.42), dimensions={1,2,3} | broadcast | bytes 18874368 | tf_op jit(solution)/shard_map/stack | solution.py:111
  147.6 0.0 copy-start.9
  147.6 5.9 %all-to-all-start = ((bf16[8,1024,2,512]{3,1,2,0:T(8,128)(2,1)}), bf16[8,1024,2,512]{3,1,2,0:T(8,128)(2,1)}, u32[]{:S(2)}, u32[]{:S(2)}) async-start(bf16[8,1024,2,512]{3,1,2,0:T(8,128)(2,1)} %stack.2), calls=%async_computation | async-start | bytes 33554432 | tf_op jit(solution)/shard_map/all_to_all | solution.py:111
  153.5 0.0 all-gather.5.cloned.1.call-start
  153.6 0.7 all-gather.5.cloned.1.call-update
  154.3 0.0 all-gather.3.cloned.1.call-start
  154.3 0.7 all-gather.3.cloned.1.call-update
  155.1 217.0 %all_gather.10 = bf16[8192,8]{0,1:T(8,128)(2,1)S(1)} all-gather(bf16[1024,8]{0,1:T(8,128)(2,1)S(1)} %copy-done.4), channel_id=1, replica_groups=mesh['wide'=32,'req'=8] {'req'}, dimensions={0}, use_global_device_ids=true | all-gather | bytes 147456 | tf_op jit(solution)/shard_map/all_gather | solution.py:117
  372.1 0.1 fusion.64
  372.2 0.1 select_reduce_fusion
  372.4 0.8 fusion.36
  373.2 0.4 fusion.57
  373.7 0.1 broadcast_multiply_fusion
  373.8 0.8 fusion.59
  374.6 4.3 reduce_sum.64
  379.0 0.0 copy-start.10
  379.0 0.0 all-gather.5.cloned.1.call-done
  379.0 51.7 %all-gather.3.cloned.1.call-done = bf16[256,8192]{1,0:T(8,128)(2,1)} async-done(((bf16[256,256]{1,0:T(8,128)(2,1)}), bf16[256,8192]{1,0:T(8,128)(2,1)}) %all-gather.3.cloned.1.call-update) | async-done | bytes 4194320 | tf_op jit(solution)/shard_map/all_gather | solution.py:103
  430.8 4.5 fusion.7
  435.3 0.3 multiply_convert_fusion.5
  435.6 0.4 collective-permute-start
  435.9 1.2 compare_select_fusion
  437.2 0.3 fusion.76
  437.4 0.3 fusion.77
  437.7 0.1 maximum_select_fusion.1
  437.7 1.2 collective-permute-start.1
  439.0 0.2 fusion.9
  439.1 3.7 collective-permute-done.1
  442.8 0.1 maximum_select_fusion
  442.9 0.7 fusion.19
  443.6 0.9 fusion.12
  444.6 0.9 fusion.44
  445.5 8.2 %copy.43 = bf16[8,1024,2,512]{3,1,0,2:T(8,128)(2,1)S(1)} copy(bf16[8,1024,2,512]{3,1,2,0:T(8,128)(2,1)} %all-to-all-done) | data formatting | bytes 33554432 | tf_op jit(solution)/shard_map/all_to_all | solution.py:111
  453.8 4.5 fusion.2
  458.3 0.9 slice_convert_fusion
  459.2 0.8 slice_bitcast_fusion
  460.0 0.8 slice_bitcast_fusion.1
  460.9 0.9 slice_bitcast_fusion.5
  461.7 2.0 copy.53
  463.8 3.0 multiply_convert_fusion.4
  466.7 1.1 copy.47
  467.8 2.2 multiply_reduce_fusion
  470.1 1.2 collective-permute-start.2
  471.3 0.8 collective-permute-done.2
  472.1 0.9 collective-permute-start.3
  473.0 1.3 convolution_add_fusion
  474.3 0.2 copy.52
  474.6 0.9 fusion.34
  (47 shorter events, 0.3 us)
Async XLA Ops:
  7.2 10.8 %copy-start = (bf16[8,3,512]{2,0,1:T(8,128)(2,1)S(1)}, bf16[8,3,512]{2,0,1:T(8,128)(2,1)}, u32[]{:S(2)}) copy-start(bf16[8,3,512]{2,0,1:T(8,128)(2,1)} %param.34) | copy-start | bytes 73732
  10.5 15.5 %all-to-all-start.2 = ((f32[16,3,128]{2,1,0:T(4,128)}), f32[16,3,128]{2,1,0:T(4,128)S(1)}, u32[]{:S(2)}, u32[]{:S(2)}) async-start(f32[16,3,128]{2,1,0:T(4,128)} %copy.48), calls=%async_computation.2 | async-start | bytes 65536 | tf_op jit(solution)/shard_map/all_to_all | solution.py:139
  26.0 15.0 %all-to-all-start.1 = ((f32[16,3,512]{2,1,0:T(4,128)}), f32[16,3,512]{2,1,0:T(4,128)S(1)}, u32[]{:S(2)}, u32[]{:S(2)}) async-start(f32[16,3,512]{2,1,0:T(4,128)} %copy.44), calls=%async_computation.1 | async-start | bytes 262144 | tf_op jit(solution)/shard_map/all_to_all | solution.py:138
  41.1 100.6 %all-to-all-start.3 = ((f32[16,8,64,256]{3,2,1,0:T(8,128)}), f32[16,8,64,256]{3,2,1,0:T(8,128)}, u32[]{:S(2)}, u32[]{:S(2)}) async-start(f32[16,8,64,256]{3,2,1,0:T(8,128)} %broadcast_select_fusion), calls=%async_computation.3 | async-start | bytes 16777216 | tf_op jit(solution)/shard_map/all_to_all | solution.py:137
  147.6 7.5 %copy-start.4 = (bf16[1024,8]{0,1:T(8,128)(2,1)S(1)}, bf16[1024,8]{0,1:T(8,128)(2,1)}, u32[]{:S(2)}) copy-start(bf16[1024,8]{0,1:T(8,128)(2,1)} %param.20) | copy-start | bytes 49156
  147.6 224.5 %copy-start.11 = (s32[1,2]{1,0:T(1,128)S(1)}, s32[1,2]{1,0:T(1,128)}, u32[]{:S(2)}) copy-start(s32[1,2]{1,0:T(1,128)} %param.30) | copy-start | bytes 28
  147.6 224.6 %copy-start.12 = (s32[2]{0:T(128)S(1)}, s32[2]{0:T(128)}, u32[]{:S(2)}) copy-start(s32[2]{0:T(128)} %param.31) | copy-start | bytes 28
  147.6 224.7 %copy-start.13 = (f32[8]{0:T(128)S(1)}, f32[8]{0:T(128)}, u32[]{:S(2)}) copy-start(f32[8]{0:T(128)} %param.23) | copy-start | bytes 100
  147.6 224.7 %copy-start.9 = (f32[4,128]{1,0:T(4,128)S(1)}, f32[4,128]{1,0:T(4,128)}, u32[]{:S(2)}) copy-start(f32[4,128]{1,0:T(4,128)} %param.27) | copy-start | bytes 6148
  147.6 224.7 %copy-start.5 = (f32[4,512]{1,0:T(4,128)S(1)}, f32[4,512]{1,0:T(4,128)}, u32[]{:S(2)}) copy-start(f32[4,512]{1,0:T(4,128)} %param.25) | copy-start | bytes 24580
  147.6 297.9 %all-to-all-start = ((bf16[8,1024,2,512]{3,1,2,0:T(8,128)(2,1)}), bf16[8,1024,2,512]{3,1,2,0:T(8,128)(2,1)}, u32[]{:S(2)}, u32[]{:S(2)}) async-start(bf16[8,1024,2,512]{3,1,2,0:T(8,128)(2,1)} %stack.2), calls=%async_computation | async-start | bytes 33554432 | tf_op jit(solution)/shard_map/all_to_all | solution.py:111
  153.5 225.5 %all-gather.5.cloned.1.call-start = ((), (), s32[]{:S(2)}) async-start(), calls=%async_computation.5 | async-start | bytes 2359296 | tf_op jit(solution)/shard_map/all_gather | solution.py:122
  154.3 276.5 %all-gather.3.cloned.1.call-start = ((), (), s32[]{:S(2)}) async-start(), calls=%async_computation.4 | async-start | bytes 4325376 | tf_op jit(solution)/shard_map/all_gather | solution.py:103
  379.0 56.3 %copy-start.10 = (f32[128]{0:T(128)S(1)}, f32[128]{0:T(128)}, u32[]{:S(2)}) copy-start(f32[128]{0:T(128)} %param.28) | copy-start | bytes 1540
  379.0 57.0 %copy-start.8 = (f32[8]{0:T(128)S(1)}, f32[8]{0:T(128)}, u32[]{:S(2)}) copy-start(f32[8]{0:T(128)} %param.22) | copy-start | bytes 100
  430.8 5.2 %copy-start.2 = (bf16[256,8192]{1,0:T(8,128)(2,1)S(1)}, bf16[256,8192]{1,0:T(8,128)(2,1)}, u32[]{:S(2)}) copy-start(bf16[256,8192]{1,0:T(8,128)(2,1)} %all-gather.3.cloned.1.call-done) | copy-start | bytes 12582916
  435.6 2.1 collective-permute-start
  437.7 5.1 %collective-permute-start.1 = (bf16[256,256]{0,1:T(8,128)(2,1)S(1)}, bf16[256,256]{0,1:T(8,128)(2,1)S(1)}, u32[]{:S(2)}, u32[]{:S(2)}) collective-permute-start(bf16[256,256]{0,1:T(8,128)(2,1)S(1)} %maximum_select_fusion.1), channel_id=1, source_target_pairs={{0,16},{16,0},{8,24},{24,8},{32,48},{48,32},{40,56},{56,40},{64,80... | collective-permute-start | bytes 393224 | tf_op jit(solution)/shard_map/ppermute | solution.py:19
  445.5 8.3 %copy-start.3 = (bf16[256,8192]{1,0:T(8,128)(2,1)S(1)}, bf16[256,8192]{1,0:T(8,128)(2,1)}, u32[]{:S(2)}) copy-start(bf16[256,8192]{1,0:T(8,128)(2,1)} %all-gather.3.cloned.1.call-done) | copy-start | bytes 12582916
  458.3 5.5 %copy-start.6 = (f32[512]{0:T(512)S(1)}, f32[512]{0:T(512)}, u32[]{:S(2)}) copy-start(f32[512]{0:T(512)} %param.26) | copy-start | bytes 6148
  459.2 8.6 %copy-start.14 = (f32[8]{0:T(128)S(1)}, f32[8]{0:T(128)}, u32[]{:S(2)}) copy-start(f32[8]{0:T(128)} %param.24) | copy-start | bytes 100
  467.8 6.7 %copy-start.7 = (f32[512]{0:T(512)S(1)}, f32[512]{0:T(512)}, u32[]{:S(2)}) copy-start(f32[512]{0:T(512)} %param.29) | copy-start | bytes 6148
  467.8 7.6 %copy-start.1 = (bf16[8,3,512]{2,0,1:T(8,128)(2,1)S(1)}, bf16[8,3,512]{2,0,1:T(8,128)(2,1)}, u32[]{:S(2)}) copy-start(bf16[8,3,512]{2,0,1:T(8,128)(2,1)} %param.34) | copy-start | bytes 73732
  470.1 2.0 collective-permute-start.2
  472.1 2.5 collective-permute-start.3
Sparse Core Ops, SparseCore 0:
  157.0 200.3 all-gather.4
  359.1 71.5 all-gather.2
